TPU v7x, 32 devices: a whole 2x2x4 slice. The times are simulated.
32 devices in a mesh: shard: 8 (over z, y), tensor: 4 (over x, core).
Axes of the slice: x: 2, y: 2, z: 4, core: 2. Of those that a mesh axis runs over, the one named last changes fastest.
Arguments:
- acts: bfloat16 [2048, 1152], P('shard', 'tensor'), may hold values from -600 to 600
- outgrads: bfloat16 [2048, 1152], P('shard', 'tensor'), may hold values from -800 to 800
- weight: bfloat16 [1152, 1152], P('shard', 'tensor'), may hold values from -6 to 6
- momentum: float32 [1152, 1152], P('shard', 'tensor'), may hold values from -6 to 6
- damping: float32 [2], replicated, may hold values from 0.3 to 3
- coeffs: float32 [4], replicated, may hold values from 0.5 to 2
Outputs:
- new_momentum: float32 [1152, 1152], P('shard', 'tensor')
- gathered_weight: bfloat16 [1152, 1152], P(None, 'tensor')
All inputs are finite; a program needn't handle non-finite values.
Results may differ from a plain program's by a relative error of at most 0.003.
The roundings to bfloat16 on the way count: a program that leaves them out, or rounds other values in their place, can miss the bound.
Values may be sent and summed in bfloat16 or wider, within the bound.
A program may use at most 64 MiB of HBM per device.

v0:
```python
import jax
import jax.numpy as jnp
from jax import lax
from jax.sharding import PartitionSpec as P

D = 1152


def horner_columns(factor, coeffs, first_col, col_count, bound_norm):
    extent = factor.shape[0]
    row_ids = lax.broadcasted_iota(jnp.int32, (extent, col_count), 0)
    col_ids = lax.broadcasted_iota(jnp.int32, (extent, col_count), 1) + first_col
    identity_cols = (row_ids == col_ids).astype(jnp.float32)
    term_count = coeffs.shape[0]
    iterate = coeffs[term_count - 1] * identity_cols
    for term_index in range(term_count - 2, -1, -1):
        product = jnp.dot(factor, iterate.astype(jnp.bfloat16), preferred_element_type=jnp.float32)
        iterate = coeffs[term_index] * identity_cols + iterate - product / bound_norm
    return iterate


def tokens_product(left, right):
    return lax.dot_general(
        left, right, (((0,), (0,)), ((), ())), preferred_element_type=jnp.float32
    )


def on_device(acts, outgrads, weight, momentum, damping, coeffs):
    row_count = weight.shape[0]
    col_count = weight.shape[1]
    row_first = lax.axis_index("shard") * row_count
    col_first = lax.axis_index("tensor") * col_count
    full_acts, full_grads = (
        lax.all_gather(acts, "tensor", axis=1, tiled=True),
        lax.all_gather(outgrads, "tensor", axis=1, tiled=True),
    )
    local_squares = jnp.stack(
        [
            jnp.sum(jnp.square(acts.astype(jnp.float32))),
            jnp.sum(jnp.square(outgrads.astype(jnp.float32))),
        ]
    )
    traces = lax.psum(local_squares, ("shard", "tensor"))
    act_part = tokens_product(full_acts, acts)
    grad_part = tokens_product(full_grads, outgrads)
    stats = lax.psum_scatter(
        jnp.concatenate([act_part, grad_part], axis=1), "shard", scatter_dimension=0, tiled=True
    )
    row_ids = lax.broadcasted_iota(jnp.int32, (row_count, col_count), 0) + row_first
    col_ids = lax.broadcasted_iota(jnp.int32, (row_count, col_count), 1) + col_first
    diag_mask = (row_ids == col_ids).astype(jnp.float32)
    act_piece = (stats[:, :col_count] + damping[0] * traces[0] / D * diag_mask).astype(jnp.bfloat16)
    grad_piece = (stats[:, col_count:] + damping[1] * traces[1] / D * diag_mask).astype(
        jnp.bfloat16
    )
    act_wide, grad_wide = (
        lax.all_gather(act_piece, "tensor", axis=1, tiled=True),
        lax.all_gather(grad_piece, "tensor", axis=1, tiled=True),
    )
    act_full, grad_full = (
        lax.all_gather(act_wide, "shard", axis=0, tiled=True),
        lax.all_gather(grad_wide, "shard", axis=0, tiled=True),
    )
    act_scale = jnp.sqrt(jnp.sum(jnp.square(act_full.astype(jnp.float32))))
    grad_scale = jnp.sqrt(jnp.sum(jnp.square(grad_full.astype(jnp.float32))))
    act_inverse = horner_columns(act_full, coeffs, row_first, row_count, act_scale)
    grad_inverse = horner_columns(grad_full, coeffs, col_first, col_count, grad_scale).astype(
        jnp.bfloat16
    )
    projected = jnp.dot(full_grads, grad_inverse, preferred_element_type=jnp.float32).astype(
        jnp.bfloat16
    )
    right_term = tokens_product(full_acts, projected)
    right_product = lax.psum(right_term, "shard")
    update = lax.dot_general(
        act_inverse,
        right_product,
        (((0,), (0,)), ((), ())),
        precision=lax.Precision.HIGHEST,
        preferred_element_type=jnp.float32,
    )
    square_sum = lax.psum(jnp.sum(update * update), ("shard", "tensor"))
    mean_square = square_sum / (D * D)
    new_momentum = 0.9 * momentum + update / jnp.sqrt(mean_square + 1e-06)
    new_weight = (weight.astype(jnp.float32) - 0.1 * new_momentum).astype(jnp.bfloat16)
    gathered_weight = lax.all_gather(new_weight, "shard", axis=0, tiled=True)
    return (new_momentum, gathered_weight)


def solution(mesh):
    in_specs = (
        P("shard", "tensor"),
        P("shard", "tensor"),
        P("shard", "tensor"),
        P("shard", "tensor"),
        P(),
        P(),
    )
    out_specs = (P("shard", "tensor"), P(None, "tensor"))
    return jax.shard_map(
        on_device, mesh=mesh, in_specs=in_specs, out_specs=out_specs, check_vma=False
    )
```

profile of v0, /device:TPU:0, one launch (start us, length us, event | category | flops | bytes accessed | tf_op | source)
XLA Modules:
  0.0 394.1 jit_solution(14097497905494058269)
XLA Ops:
  7.2 9.2 %all_gather.21 = bf16[256,1152]{0,1:T(8,128)(2,1)S(1)} all-gather(bf16[256,288]{0,1:T(8,128)(2,1)} %param.6), channel_id=1, replica_groups=mesh['shard'=8,'tensor'=4] {'tensor'}, dimensions={1}, use_global_device_ids=true | all-gather | bytes 737280 | tf_op jit(solution)/shard_map/all_gather | solution.py:34
  16.4 1.3 fusion.37
  17.7 7.6 %all_gather.22 = bf16[256,1152]{0,1:T(8,128)(2,1)S(1)} all-gather(bf16[256,288]{0,1:T(8,128)(2,1)S(1)} %copy-done.4), channel_id=1, replica_groups=mesh['shard'=8,'tensor'=4] {'tensor'}, dimensions={1}, use_global_device_ids=true | all-gather | bytes 737280 | tf_op jit(solution)/shard_map/all_gather | solution.py:35
  26.7 2.3 copy.17
  31.4 1.4 pad_maximum_fusion.1
  32.7 41.5 %psum.21 = f32[2]{0:T(128)S(1)} all-reduce(f32[2]{0:T(128)S(1)} %pad_maximum_fusion.1), channel_id=1, replica_groups=mesh['shard'=8,'tensor'=4] {'shard','tensor'}, use_global_device_ids=true, to_apply=%region_3.0 | all-reduce | flops 2 | bytes 16 | tf_op jit(solution)/shard_map/psum | solution.py:43
  78.0 25.5 %reduce-scatter.4.cloned.1.call-done = f32[144,576]{1,0:T(8,128)} async-done(((f32[1152,576]{1,0:T(8,128)}), f32[144,576]{1,0:T(8,128)}) %reduce-scatter.4.cloned.1.call-update) | async-done | bytes 331792
  105.2 6.7 %all-gather.1 = bf16[4,288,144]{1,2,0:T(8,128)(2,1)S(1)} all-gather(bf16[1,288,144]{1,2,0:T(8,128)(2,1)S(1)} %copy.14), channel_id=1, replica_groups=mesh['shard'=8,'tensor'=4] {'tensor'}, dimensions={0}, use_global_device_ids=true | all-gather | bytes 414720 | tf_op jit(solution)/shard_map/all_gather | solution.py:58
  113.3 6.8 %all-gather = bf16[4,288,144]{1,2,0:T(8,128)(2,1)S(1)} all-gather(bf16[1,288,144]{1,2,0:T(8,128)(2,1)S(1)} %copy.12), channel_id=1, replica_groups=mesh['shard'=8,'tensor'=4] {'tensor'}, dimensions={0}, use_global_device_ids=true | all-gather | bytes 414720 | tf_op jit(solution)/shard_map/all_gather | solution.py:57
  122.3 44.7 %all-gather.7.cloned.1.call-done = bf16[1152,1152]{1,0:T(8,128)(2,1)} async-done(((bf16[144,1152]{1,0:T(8,128)(2,1)}), bf16[1152,1152]{1,0:T(8,128)(2,1)}) %all-gather.7.cloned.1.call-update) | async-done | bytes 2654224 | tf_op jit(solution)/shard_map/all_gather | solution.py:62
  167.0 3.9 multiply_reduce_fusion
  171.6 2.4 fusion.2
  174.1 2.9 fusion.1
  177.0 3.9 fusion.8
  180.9 1.5 convolution_bitcast_fusion
  182.3 40.7 %all-gather.5.cloned.1.call-done = bf16[1152,1152]{1,0:T(8,128)(2,1)} async-done(((bf16[144,1152]{1,0:T(8,128)(2,1)}), bf16[1152,1152]{1,0:T(8,128)(2,1)}) %all-gather.5.cloned.1.call-update) | async-done | bytes 2654224 | tf_op jit(solution)/shard_map/all_gather | solution.py:61
  223.1 3.9 multiply_reduce_fusion.1
  227.7 2.2 fusion.4
  229.9 1.6 fusion.5
  231.5 1.6 fusion.6
  233.1 75.8 %all-reduce.2.cloned.1.call-done = f32[1152,288]{0,1:T(8,128)} async-done(((f32[1152,288]{0,1:T(8,128)}), f32[1152,288]{0,1:T(8,128)}) %all-reduce.2.cloned.1.call-update) | async-done | bytes 1327120 | tf_op jit(solution)/shard_map/psum | solution.py:74
  308.9 3.7 multiply_reduce_fusion.4
  312.5 40.0 %psum.23 = f32[]{:T(128)} all-reduce(f32[]{:T(128)} %get-tuple-element.22), channel_id=1, replica_groups=mesh['shard'=8,'tensor'=4] {'shard','tensor'}, use_global_device_ids=true, to_apply=%region_8.0 | all-reduce | flops 1 | bytes 8 | tf_op jit(solution)/shard_map/psum | solution.py:82
  354.0 32.4 %all_gather.27 = bf16[1152,288]{1,0:T(8,128)(2,1)S(1)} all-gather(bf16[144,288]{1,0:T(8,128)(2,1)S(1)} %get-tuple-element.8), channel_id=1, replica_groups=mesh['shard'=8,'tensor'=4] {'shard'}, dimensions={0}, use_global_device_ids=true | all-gather | bytes 746496 | tf_op jit(solution)/shard_map/all_gather | solution.py:86
  (47 shorter events, 12.0 us)
Async XLA Ops:
  7.2 10.5 %copy-start.4 = (bf16[256,288]{0,1:T(8,128)(2,1)S(1)}, bf16[256,288]{0,1:T(8,128)(2,1)}, u32[]{:S(2)}) copy-start(bf16[256,288]{0,1:T(8,128)(2,1)} %param.7) | copy-start | bytes 442372
  7.2 96.3 %reduce-scatter.4.cloned.1.call-start = ((), (), s32[]{:S(2)}) async-start(), calls=%async_computation.4 | async-start | bytes 3317760
  25.4 0.8 copy-start.2
  29.1 0.9 copy-start.3
  29.1 45.8 %copy-start.8 = (f32[2]{0:T(128)S(1)}, f32[2]{0:T(128)}, u32[]{:S(2)}) copy-start(f32[2]{0:T(128)} %param.10) | copy-start | bytes 28
  29.1 137.9 %all-gather.7.cloned.1.call-start = ((), (), s32[]{:S(2)}) async-start(), calls=%async_computation.2 | async-start | bytes 2985984 | tf_op jit(solution)/shard_map/all_gather | solution.py:62
  113.1 110.0 %all-gather.5.cloned.1.call-start = ((), (), s32[]{:S(2)}) async-start(), calls=%async_computation.1 | async-start | bytes 2985984 | tf_op jit(solution)/shard_map/all_gather | solution.py:61
  113.3 8.3 %copy-start.7 = (f32[4]{0:T(128)S(1)}, f32[4]{0:T(128)}, u32[]{:S(2)}) copy-start(f32[4]{0:T(128)} %param.11) | copy-start | bytes 52
  121.4 187.4 %all-reduce.2.cloned.1.call-start = ((), (), s32[]{:S(2)}) async-start(), calls=%async_computation.3 | async-start | bytes 2654208 | tf_op jit(solution)/shard_map/psum | solution.py:74
  167.0 4.6 %copy-start.1 = (bf16[1152,1152]{1,0:T(8,128)(2,1)S(1)}, bf16[1152,1152]{1,0:T(8,128)(2,1)}, u32[]{:S(2)}) copy-start(bf16[1152,1152]{1,0:T(8,128)(2,1)} %all-gather.7.cloned.1.call-done) | copy-start | bytes 7962628
  223.1 4.6 %copy-start = (bf16[1152,1152]{1,0:T(8,128)(2,1)S(1)}, bf16[1152,1152]{1,0:T(8,128)(2,1)}, u32[]{:S(2)}) copy-start(bf16[1152,1152]{1,0:T(8,128)(2,1)} %all-gather.5.cloned.1.call-done) | copy-start | bytes 7962628
  233.1 120.2 %copy-start.5 = (f32[144,288]{1,0:T(8,128)S(1)}, f32[144,288]{1,0:T(8,128)}, u32[]{:S(2)}) copy-start(f32[144,288]{1,0:T(8,128)} %param.9) | copy-start | bytes 497668
  233.1 120.2 %copy-start.6 = (bf16[144,288]{1,0:T(8,128)(2,1)S(1)}, bf16[144,288]{1,0:T(8,128)(2,1)}, u32[]{:S(2)}) copy-start(bf16[144,288]{1,0:T(8,128)(2,1)} %param.8) | copy-start | bytes 248836
Sparse Core Ops, SparseCore 0:
  29.2 74.2 reduce-scatter.3
  113.2 53.7 all-gather.6
  169.4 53.5 all-gather.4
  226.9 81.9 all-reduce.1
where the time goes:
time: 395 us; the launch traced here: 394 us
  waiting for transfers between devices  187 us (47%)
  blocking collectives  144 us (36%)
  matrix products  21.4 us (5%)
  between operations  18.6 us (5%)
  other arithmetic  11.5 us (3%)
  local copies, waits for them, and re-layouts  11.1 us (3%)
    psum x1, waiting for transfers between devices, on_device(): right_product = lax.psum(right_term, 'shard')  75.8 us
    all_gather x1, waiting for transfers between devices, on_device(): lax.all_gather(grad_wide, 'shard', axis=0, tiled=True)  44.7 us
    psum x1, blocking collectives, on_device(): traces = lax.psum(local_squares, ('shard', 'tensor'))  41.5 us
    all_gather x1, waiting for transfers between devices, on_device(): lax.all_gather(act_wide, 'shard', axis=0, tiled=True)  40.7 us
    psum x1, blocking collectives, on_device(): square_sum = lax.psum(jnp.sum(update * update), ('shard', 'tensor'))  40 us
    all_gather x1, blocking collectives, on_device(): gathered_weight = lax.all_gather(new_weight, 'shard', axis=0, tiled=True)  32.4 us
    unnamed x5, waiting for transfers between devices  25.6 us
    dot_general x5, matrix products, horner_columns(): jnp.dot(factor, iterate.astype(jnp.bfloat16), preferred_element_type=jnp....  10.7 us
  transfers between devices with their start and end apart: 4, of which 4 were waited for; matrix products, arithmetic and copies ran while one was open for 8% of the time, Pallas kernels for 0%

commit v1 on v0

--- a/solution.py
+++ b/solution.py
@@ -1,6 +1,10 @@
+import functools
+
 import jax
 import jax.numpy as jnp
 from jax import lax
+from jax.experimental import pallas as pl
+from jax.experimental.pallas import tpu as pltpu
 from jax.sharding import PartitionSpec as P
 
 D = 1152
@@ -87,6 +91,411 @@
     return (new_momentum, gathered_weight)
 
 
+MESH = pl.DeviceIdType.MESH
+BF16 = jnp.bfloat16
+F32 = jnp.float32
+Y_CHIPS = 2
+CORES = 2
+TILES = 3
+
+
+def dot_nt(left, right):
+    return lax.dot_general(
+        left, right, (((1,), (1,)), ((), ())), preferred_element_type=jnp.float32
+    )
+
+
+def dot_nn(left, right, precision=None):
+    return lax.dot_general(
+        left,
+        right,
+        (((1,), (0,)), ((), ())),
+        precision=precision,
+        preferred_element_type=jnp.float32,
+    )
+
+
+def eye(rows, cols, row_first, col_first):
+    row_ids = lax.broadcasted_iota(jnp.int32, (rows, cols), 0) + row_first
+    col_ids = lax.broadcasted_iota(jnp.int32, (rows, cols), 1) + col_first
+    return row_ids == col_ids
+
+
+def total(value):
+    return jnp.sum(jnp.sum(value, axis=0, keepdims=True), axis=1, keepdims=True)
+
+
+class Place:
+    def __init__(self, shards):
+        self.depth = shards // Y_CHIPS
+        self.s = lax.axis_index("shard")
+        self.t = lax.axis_index("tensor")
+        self.z, self.y = self.s // Y_CHIPS, self.s % Y_CHIPS
+        self.x, self.c = self.t // CORES, self.t % CORES
+        c = self.c
+        self.y2 = c * self.y + (1 - c) * (1 - self.y)
+        self.x2 = (1 - c) * self.x + c * (1 - self.x)
+        self.y3 = (1 - c) * self.y + c * (1 - self.y)
+        self.x3 = c * self.x + (1 - c) * (1 - self.x)
+
+    def id(self, z, y, x, c):
+        return (z * Y_CHIPS + y, x * CORES + c)
+
+    def z_at(self, k):
+        return (self.z - k + self.depth) % self.depth
+
+
+class Stream:
+    def __init__(self, place, buf, width, sems):
+        self.p, self.buf, self.width, self.sems = place, buf, width, sems
+        self.n = place.depth
+        self.sends = []
+
+    def block(self, z, y, x, c):
+        rows = pl.multiple_of((x * CORES + c) * self.width, self.width)
+        return self.buf.at[z * Y_CHIPS + y, pl.ds(rows, self.width), :]
+
+    def copy(self, kind, index, where, target):
+        ref = self.block(*where)
+        send, recv = self.sems[kind]
+        return pltpu.make_async_remote_copy(
+            src_ref=ref,
+            dst_ref=ref,
+            send_sem=send.at[index],
+            recv_sem=recv.at[index],
+            device_id=target,
+            device_id_type=MESH,
+        )
+
+    def send(self, kind, index, where, target):
+        copy = self.copy(kind, index, where, target)
+        copy.start()
+        self.sends.append(copy)
+
+    def arrive(self, kind, index, where):
+        p = self.p
+        self.copy(kind, index, where, p.id(p.z, p.y, p.x, 1 - p.c)).wait_recv()
+
+    def to_second(self, k, where):
+        p = self.p
+        self.send("second", k, where, p.id(p.z, p.y2, p.x2, p.c))
+
+    def to_third(self, k, where):
+        p = self.p
+        self.send("third", k, where, p.id(p.z, p.y3, p.x3, p.c))
+
+    def to_sibling(self, k, where):
+        p = self.p
+        self.send("sibling", k, where, p.id(p.z, p.y, p.x, 1 - p.c))
+
+    def start(self):
+        p = self.p
+        own = (p.z, p.y, p.x, p.c)
+        for k in range(1, self.n):
+            self.send("line", k - 1, own, p.id((p.z + k) % self.n, p.y, p.x, p.c))
+        self.to_second(0, own)
+        self.to_third(0, own)
+        self.to_sibling(0, own)
+
+    def line(self, k):
+        p = self.p
+        where = (p.z_at(k), p.y, p.x, p.c)
+        self.arrive("line", k - 1, where)
+        self.to_second(k, where)
+        self.to_third(k, where)
+        self.to_sibling(k, where)
+
+    def second(self, k):
+        p = self.p
+        where = (p.z_at(k), p.y2, p.x2, p.c)
+        self.arrive("second", k, where)
+        self.to_third(self.n + k, where)
+        self.to_sibling(self.n + k, where)
+
+    def third(self, k):
+        p = self.p
+        if k < self.n:
+            where = (p.z_at(k), p.y3, p.x3, p.c)
+        else:
+            where = (p.z_at(k - self.n), 1 - p.y, 1 - p.x, p.c)
+        self.arrive("third", k, where)
+        self.to_sibling(2 * self.n + k, where)
+
+    def sibling(self):
+        p = self.p
+        o = 1 - p.c
+        y2, x2, y3, x3 = p.y3, p.x3, p.y2, p.x2
+        for k in range(self.n):
+            self.arrive("sibling", k, (p.z_at(k), p.y, p.x, o))
+        for k in range(self.n):
+            self.arrive("sibling", self.n + k, (p.z_at(k), y2, x2, o))
+        for k in range(self.n):
+            self.arrive("sibling", 2 * self.n + k, (p.z_at(k), y3, x3, o))
+        for k in range(self.n):
+            self.arrive("sibling", 3 * self.n + k, (p.z_at(k), 1 - p.y, 1 - p.x, o))
+
+    def finish(self):
+        for copy in self.sends:
+            copy.wait_send()
+
+
+def cov_rows(buf, cov, i):
+    slabs, d, _ = buf.shape
+    tile = d // TILES
+    left = jnp.concatenate([buf[k, i * tile : (i + 1) * tile, :] for k in range(slabs)], axis=1)
+
+    def column(j, carry):
+        first = pl.multiple_of(j * tile, tile)
+        right = jnp.concatenate([buf[k, pl.ds(first, tile), :] for k in range(slabs)], axis=1)
+        cov[i * tile : (i + 1) * tile, pl.ds(first, tile)] = dot_nt(left, right)
+        return carry
+
+    lax.fori_loop(0, TILES, column, 0)
+
+
+def damp(cov, factor, damping):
+    d = cov.shape[0]
+    step = d // 9
+    trace = jnp.zeros((1, 1), F32)
+    for i in range(9):
+        part = cov[i * step : (i + 1) * step, i * step : (i + 1) * step]
+        trace = trace + total(jnp.where(eye(step, step, 0, 0), part, 0.0))
+    shift = damping * trace / d
+
+    def rows(i, acc):
+        first = pl.multiple_of(i * step, step)
+        piece = cov[pl.ds(first, step), :]
+        diag = eye(step, d, first, 0)
+        piece = (piece + jnp.where(diag, shift, 0.0)).astype(BF16)
+        factor[pl.ds(first, step), :] = piece
+        wide = piece.astype(F32)
+        return acc + jnp.sum(wide * wide, axis=0, keepdims=True)
+
+    squares = lax.fori_loop(0, 9, rows, jnp.zeros((1, d), F32))
+    return jnp.sqrt(jnp.sum(squares, axis=1, keepdims=True))
+
+
+def horner_rows(factor, work, coeffs, first, norm):
+    rows, d = work.shape
+    tile = d // TILES
+    terms = coeffs.shape[0]
+    inv = 1.0 / norm
+    start = pl.multiple_of(first, rows)
+    top = jnp.full((1, 1), coeffs[terms - 1], F32).astype(BF16).astype(F32)
+    diag = eye(rows, d, first, 0)
+    value = jnp.where(diag, coeffs[terms - 2] + coeffs[terms - 1], 0.0)
+    work[...] = value - factor[pl.ds(start, rows), :].astype(F32) * top * inv
+    for term in range(terms - 3, -1, -1):
+        low = work[...].astype(BF16)
+        for j in range(TILES):
+            cols = slice(j * tile, (j + 1) * tile)
+            product = dot_nn(low, factor[:, cols])
+            held = jnp.where(eye(rows, tile, first, j * tile), coeffs[term], 0.0)
+            work[:, cols] = held + work[:, cols] - product * inv
+
+
+def step_kernel(
+    shards,
+    acts_ref,
+    grads_ref,
+    weight_ref,
+    momentum_ref,
+    damping_ref,
+    coeffs_ref,
+    new_momentum_ref,
+    gathered_ref,
+    acts_all,
+    grads_all,
+    cov,
+    factor,
+    grad_work,
+    grad_low,
+    act_work,
+    projected,
+    right,
+    weight_all,
+    shard_sums,
+    tensor_sums,
+    *sems,
+):
+    p = Place(shards)
+    n = p.depth
+    s, t = p.s, p.t
+    tensors = grads_all.shape[1] // grads_ref.shape[1]
+    width = grads_ref.shape[1]
+    barrier = pltpu.get_barrier_semaphore()
+    peers = [((s + k) % shards, t) for k in range(1, shards)]
+    peers += [(s, (t + k) % tensors) for k in range(1, tensors)]
+    for peer in peers:
+        pl.semaphore_signal(barrier, inc=1, device_id=peer, device_id_type=MESH)
+
+    kinds = ("line", "second", "third", "sibling")
+    pairs = list(zip(sems[0::2], sems[1::2]))
+    grads = Stream(p, grads_all, width, dict(zip(kinds, pairs[0:4])))
+    acts = Stream(p, acts_all, width, dict(zip(kinds, pairs[4:8])))
+    ones = eye(width, width, 0, 0).astype(F32).astype(BF16)
+    own_rows = pl.ds(pl.multiple_of(t * width, width), width)
+    grads_all[s, own_rows, :] = dot_nt(ones, grads_ref[...]).astype(BF16)
+    acts_all[s, own_rows, :] = dot_nt(ones, acts_ref[...]).astype(BF16)
+    pl.semaphore_wait(barrier, len(peers))
+
+    grads.start()
+    for k in range(1, n):
+        grads.line(k)
+        grads.second(k - 1)
+    grads.second(n - 1)
+    acts.start()
+    for k in range(1, n):
+        acts.line(k)
+        acts.second(k - 1)
+        grads.third(2 * k - 2)
+        grads.third(2 * k - 1)
+    acts.second(n - 1)
+    for k in range(2 * n - 2, 2 * n):
+        grads.third(k)
+    grads.sibling()
+    third = 0
+    for i in range(TILES):
+        cov_rows(grads_all, cov, i)
+        acts.third(third)
+        third += 1
+    grad_norm = damp(cov, factor, damping_ref[1])
+    while third < n:
+        acts.third(third)
+        third += 1
+    horner_rows(factor, grad_work, coeffs_ref, t * width, grad_norm)
+    grad_low[...] = grad_work[...].astype(BF16)
+    acts.third(third)
+    third += 1
+
+    def project(k, carry):
+        projected[k] = dot_nn(grad_low[...], grads_all[k]).astype(BF16)
+        return carry
+
+    lax.fori_loop(0, shards, project, 0)
+    while third < 2 * n:
+        acts.third(third)
+        third += 1
+    acts.sibling()
+    for i in range(TILES):
+        cov_rows(acts_all, cov, i)
+    act_norm = damp(cov, factor, damping_ref[0])
+    height = weight_ref.shape[0]
+    horner_rows(factor, act_work, coeffs_ref, s * height, act_norm)
+    tile = cov.shape[0] // TILES
+    low = jnp.concatenate([projected[k] for k in range(shards)], axis=1)
+
+    def right_rows(i, carry):
+        first = pl.multiple_of(i * tile, tile)
+        left = jnp.concatenate(
+            [acts_all[k, pl.ds(first, tile), :] for k in range(shards)], axis=1
+        )
+        right[pl.ds(first, tile), :] = dot_nt(left, low)
+        return carry
+
+    lax.fori_loop(0, TILES, right_rows, 0)
+    update = dot_nn(act_work[...], right[...], lax.Precision.HIGHEST)
+
+    started = []
+
+    def push(src, dst, pair, index, target):
+        copy = pltpu.make_async_remote_copy(
+            src_ref=src,
+            dst_ref=dst,
+            send_sem=pair[0].at[index],
+            recv_sem=pair[1].at[index],
+            device_id=target,
+            device_id_type=MESH,
+        )
+        copy.start()
+        started.append(copy)
+        return copy
+
+    shard_sums[s] = jnp.broadcast_to(total(update * update), shard_sums.shape[1:])
+    copies = [
+        push(shard_sums.at[s], shard_sums.at[s], pairs[8], k - 1, ((s + k) % shards, t))
+        for k in range(1, shards)
+    ]
+    for copy in copies:
+        copy.wait_recv()
+    tensor_sums[t] = jnp.sum(shard_sums[...], axis=0)
+    copies = [
+        push(tensor_sums.at[t], tensor_sums.at[t], pairs[9], k - 1, (s, (t + k) % tensors))
+        for k in range(1, tensors)
+    ]
+    for copy in copies:
+        copy.wait_recv()
+    square_sum = jnp.sum(tensor_sums[...], axis=0)[0:1, 0:1]
+    d = cov.shape[0]
+    mean_square = square_sum / (d * d)
+    momentum = 0.9 * momentum_ref[...] + update / jnp.sqrt(mean_square + 1e-06)
+    new_momentum_ref[...] = momentum
+    new_weight = weight_ref[...].astype(F32) - 0.1 * momentum
+
+    def rows_of(z, y):
+        return weight_all.at[pl.ds(pl.multiple_of((z * Y_CHIPS + y) * height, height), height), :]
+
+    weight_all[pl.ds(pl.multiple_of(s * height, height), height), :] = new_weight.astype(BF16)
+    own = rows_of(p.z, p.y)
+    across = (p.z * Y_CHIPS + 1 - p.y, t)
+    lines = [
+        push(own, own, pairs[10], k - 1, (((p.z + k) % n) * Y_CHIPS + p.y, t))
+        for k in range(1, n)
+    ]
+    crossed = [push(own, own, pairs[11], 0, across)]
+    for k in range(1, n):
+        lines[k - 1].wait_recv()
+        piece = rows_of(p.z_at(k), p.y)
+        crossed.append(push(piece, piece, pairs[11], k, across))
+    for copy in crossed:
+        copy.wait_recv()
+    gathered_ref[...] = weight_all[...]
+    for copy in started:
+        copy.wait_send()
+    grads.finish()
+    acts.finish()
+
+
+def on_device_whole(shards, tensors, acts, outgrads, weight, momentum, damping, coeffs):
+    tokens, width = acts.shape
+    height = weight.shape[0]
+    d = width * tensors
+    n = shards // Y_CHIPS
+    vmem = pl.BlockSpec(memory_space=pltpu.VMEM)
+    smem = pl.BlockSpec(memory_space=pltpu.SMEM)
+    counts = [n - 1, n, 2 * n, 4 * n] * 2 + [shards - 1, tensors - 1, n - 1, n]
+    sems = []
+    for count in counts:
+        sems += [pltpu.SemaphoreType.DMA((count,))] * 2
+    return pl.pallas_call(
+        functools.partial(step_kernel, shards),
+        out_shape=(
+            jax.ShapeDtypeStruct((height, width), F32),
+            jax.ShapeDtypeStruct((d, width), BF16),
+        ),
+        in_specs=[vmem, vmem, vmem, vmem, smem, smem],
+        out_specs=(vmem, vmem),
+        scratch_shapes=[
+            pltpu.VMEM((shards, d, tokens), BF16),
+            pltpu.VMEM((shards, d, tokens), BF16),
+            pltpu.VMEM((d, d), F32),
+            pltpu.VMEM((d, d), BF16),
+            pltpu.VMEM((width, d), F32),
+            pltpu.VMEM((width, d), BF16),
+            pltpu.VMEM((height, d), F32),
+            pltpu.VMEM((shards, width, tokens), BF16),
+            pltpu.VMEM((d, width), F32),
+            pltpu.VMEM((d, width), BF16),
+            pltpu.VMEM((shards, 8, 128), F32),
+            pltpu.VMEM((tensors, 8, 128), F32),
+        ]
+        + sems,
+        compiler_params=pltpu.CompilerParams(
+            collective_id=0, has_side_effects=True, vmem_limit_bytes=56 * 2**20
+        ),
+    )(acts, outgrads, weight, momentum, damping, coeffs)
+
+
 def solution(mesh):
     in_specs = (
         P("shard", "tensor"),
@@ -97,6 +506,14 @@
         P(),
     )
     out_specs = (P("shard", "tensor"), P(None, "tensor"))
+    shards, tensors = mesh.shape["shard"], mesh.shape["tensor"]
+
+    def local(acts, *rest):
+        held = 2 * acts.dtype.itemsize * acts.size * shards * tensors
+        if held <= 24 * 2**20:
+            return on_device_whole(shards, tensors, acts, *rest)
+        return on_device(acts, *rest)
+
     return jax.shard_map(
-        on_device, mesh=mesh, in_specs=in_specs, out_specs=out_specs, check_vma=False
-    )
+        local, mesh=mesh, in_specs=in_specs, out_specs=out_specs, check_vma=False
+    )

time: 395 us -> 116 us (0.29)
  waiting for transfers between devices: 187 us -> 0 us
  blocking collectives: 144 us -> 0 us
  Pallas kernels: 0 us -> 110 us
  matrix products: 21.4 us -> 0 us
  between operations: 18.6 us -> 0.66 us
  other arithmetic: 11.5 us -> 0 us
  local copies, waits for them, and re-layouts: 11.1 us -> 5.6 us
    pallas_call x0 -> x1, Pallas kernels: none -> 110 us  [on_device_whole(): pl.pallas_call(functools.partial(step_kernel, shards), out_shape=(jax.Sha...]
    all_gather x2 -> x0, waiting for transfers between devices: 85.5 us -> none  [the longest x1 44.7 us: on_device(): lax.all_gather(grad_wide, 'shard', axis=0, tiled=True)]
    psum x2 -> x0, blocking collectives: 81.6 us -> none  [the longest x1 41.5 us: on_device(): traces = lax.psum(local_squares, ('shard', 'tensor'))]
    psum x1 -> x0, waiting for transfers between devices: 75.8 us -> none  [on_device(): right_product = lax.psum(right_term, 'shard')]
    all_gather x5 -> x0, blocking collectives: 62.7 us -> none  [the longest x1 32.4 us: on_device(): gathered_weight = lax.all_gather(new_weight, 'shard', axis=0, tiled=True)]
    unnamed x5 -> x0, waiting for transfers between devices: 25.6 us -> none
    dot_general x10 -> x0, matrix products: 21.4 us -> none  [the longest x5 10.7 us: horner_columns(): jnp.dot(factor, iterate.astype(jnp.bfloat16), preferred_element_type=jnp....]
    reduce_sum x4 -> x0, other arithmetic: 9.11 us -> none  [the longest x1 3.87 us: on_device(): grad_scale = jnp.sqrt(jnp.sum(jnp.square(grad_full.astype(jnp.float32))))]
  transfers between devices with their start and end apart: 4 -> 0, of which waited for: 4 -> 0; matrix products, arithmetic and copies ran while one was open for 8% -> 0% of each run, Pallas kernels for 0% -> 0%
where the time goes in v1:
time: 116 us
  Pallas kernels  110 us (95%)
  local copies, waits for them, and re-layouts  5.6 us (5%)
    pallas_call x1, Pallas kernels, on_device_whole(): pl.pallas_call(functools.partial(step_kernel, shards), out_shape=(jax.Sha...  110 us
    unnamed x7, local copies, waits for them, and re-layouts  3.27 us
    pallas_call x1, local copies, waits for them, and re-layouts, on_device_whole(): pl.pallas_call(functools.partial(step_kernel, shards), out_shape=(jax.Sha...  2.33 us

profile of v1, /device:TPU:0, one launch (start us, length us, event | category | flops | bytes accessed | tf_op | source)
XLA Modules:
  0.0 116.0 jit_solution(17018318274518630239)
XLA Ops:
  0.6 0.0 copy-start.1
  0.6 1.8 %copy.8.acts_ref = bf16[256,288]{1,0:T(8,128)(2,1)} copy(bf16[256,288]{0,1:T(8,128)(2,1)} %param.6) | data formatting | bytes 294912 | tf_op args[0]
  2.4 0.0 copy-done.1
  2.4 0.8 copy.9.grads_ref
  3.2 109.8 %shard_map.77 = (f32[144,288]{1,0:T(8,128)}, bf16[1152,288]{1,0:T(8,128)(2,1)}) custom-call(bf16[256,288]{1,0:T(8,128)(2,1)} %copy.8.acts_ref, bf16[256,288]{1,0:T(8,128)(2,1)} %copy.9.grads_ref, bf16[144,288]{1,0:T(8,128)(2,1)} %weight_ref.1, f32[144,288]{1,0:T(8,128)} %momentum_ref.1, f32[2]{0:T(128)} %damping_ref.1, f32[4]{0:T(128)} %coeffs_ref.1), custom_call_target="tpu_custom_call" | custom-call | tf_op jit(solution)/shard_map/pallas_call | solution.py:470
  113.0 0.0 copy-start
  113.0 2.3 %copy.10 = bf16[1152,288]{0,1:T(8,128)(2,1)} copy(bf16[1152,288]{1,0:T(8,128)(2,1)} %get-tuple-element.3) | data formatting | bytes 1327104 | tf_op jit(solution)/shard_map/pallas_call | solution.py:470
  115.3 0.0 copy-done
  115.3 0.7 copy.12
Async XLA Ops:
  0.6 1.8 %copy-start.1 = (bf16[256,288]{0,1:T(8,128)(2,1)S(1)}, bf16[256,288]{0,1:T(8,128)(2,1)}, u32[]{:S(2)}) copy-start(bf16[256,288]{0,1:T(8,128)(2,1)} %param.7) | copy-start | bytes 442372
  113.0 2.3 %copy-start = (f32[144,288]{1,0:T(8,128)S(1)}, f32[144,288]{1,0:T(8,128)}, u32[]{:S(2)}) copy-start(f32[144,288]{1,0:T(8,128)} %get-tuple-element.6) | copy-start | bytes 497668

commit v2 on v1

--- a/solution.py
+++ b/solution.py
@@ -221,36 +221,27 @@
         self.arrive("third", k, where)
         self.to_sibling(2 * self.n + k, where)
 
-    def sibling(self):
-        p = self.p
-        o = 1 - p.c
-        y2, x2, y3, x3 = p.y3, p.x3, p.y2, p.x2
-        for k in range(self.n):
-            self.arrive("sibling", k, (p.z_at(k), p.y, p.x, o))
-        for k in range(self.n):
-            self.arrive("sibling", self.n + k, (p.z_at(k), y2, x2, o))
-        for k in range(self.n):
-            self.arrive("sibling", 2 * self.n + k, (p.z_at(k), y3, x3, o))
-        for k in range(self.n):
-            self.arrive("sibling", 3 * self.n + k, (p.z_at(k), 1 - p.y, 1 - p.x, o))
+    def sibling(self, first, last):
+        p = self.p
+        where = [(p.y, p.x), (p.y3, p.x3), (p.y2, p.x2), (1 - p.y, 1 - p.x)]
+        for k in range(first, last):
+            y, x = where[k // self.n]
+            self.arrive("sibling", k, (p.z_at(k % self.n), y, x, 1 - p.c))
 
     def finish(self):
         for copy in self.sends:
             copy.wait_send()
 
 
-def cov_rows(buf, cov, i):
-    slabs, d, _ = buf.shape
-    tile = d // TILES
-    left = jnp.concatenate([buf[k, i * tile : (i + 1) * tile, :] for k in range(slabs)], axis=1)
-
-    def column(j, carry):
-        first = pl.multiple_of(j * tile, tile)
-        right = jnp.concatenate([buf[k, pl.ds(first, tile), :] for k in range(slabs)], axis=1)
-        cov[i * tile : (i + 1) * tile, pl.ds(first, tile)] = dot_nt(left, right)
-        return carry
-
-    lax.fori_loop(0, TILES, column, 0)
+def lanes(buf, slabs, rows):
+    return jnp.concatenate([buf[k, rows, :] for k in slabs], axis=1)
+
+
+def cov_tile(buf, cov, slabs, i, j, add):
+    tile = cov.shape[0] // TILES
+    rows, cols = pl.ds(i * tile, tile), pl.ds(j * tile, tile)
+    product = dot_nt(lanes(buf, slabs, rows), lanes(buf, slabs, cols))
+    cov[rows, cols] = cov[rows, cols] + product if add else product
 
 
 def damp(cov, factor, damping):
@@ -275,23 +266,28 @@
     return jnp.sqrt(jnp.sum(squares, axis=1, keepdims=True))
 
 
-def horner_rows(factor, work, coeffs, first, norm):
+def horner_steps(factor, work, coeffs, first, norm):
     rows, d = work.shape
     tile = d // TILES
     terms = coeffs.shape[0]
-    inv = 1.0 / norm
-    start = pl.multiple_of(first, rows)
-    top = jnp.full((1, 1), coeffs[terms - 1], F32).astype(BF16).astype(F32)
-    diag = eye(rows, d, first, 0)
-    value = jnp.where(diag, coeffs[terms - 2] + coeffs[terms - 1], 0.0)
-    work[...] = value - factor[pl.ds(start, rows), :].astype(F32) * top * inv
-    for term in range(terms - 3, -1, -1):
+
+    def begin():
+        start = pl.multiple_of(first, rows)
+        top = jnp.full((1, 1), coeffs[terms - 1], F32).astype(BF16).astype(F32)
+        diag = eye(rows, d, first, 0)
+        value = jnp.where(diag, coeffs[terms - 2] + coeffs[terms - 1], 0.0)
+        work[...] = value - factor[pl.ds(start, rows), :].astype(F32) * (top / norm())
+
+    def term(index):
         low = work[...].astype(BF16)
+        inv = 1.0 / norm()
         for j in range(TILES):
             cols = slice(j * tile, (j + 1) * tile)
             product = dot_nn(low, factor[:, cols])
-            held = jnp.where(eye(rows, tile, first, j * tile), coeffs[term], 0.0)
+            held = jnp.where(eye(rows, tile, first, j * tile), coeffs[index], 0.0)
             work[:, cols] = held + work[:, cols] - product * inv
+
+    return [begin] + [functools.partial(term, k) for k in range(terms - 3, -1, -1)]
 
 
 def step_kernel(
@@ -321,8 +317,8 @@
     p = Place(shards)
     n = p.depth
     s, t = p.s, p.t
-    tensors = grads_all.shape[1] // grads_ref.shape[1]
-    width = grads_ref.shape[1]
+    tensors = grads_all.shape[1] // grads_ref.shape[0]
+    width = grads_ref.shape[0]
     barrier = pltpu.get_barrier_semaphore()
     peers = [((s + k) % shards, t) for k in range(1, shards)]
     peers += [(s, (t + k) % tensors) for k in range(1, tensors)]
@@ -333,10 +329,9 @@
     pairs = list(zip(sems[0::2], sems[1::2]))
     grads = Stream(p, grads_all, width, dict(zip(kinds, pairs[0:4])))
     acts = Stream(p, acts_all, width, dict(zip(kinds, pairs[4:8])))
-    ones = eye(width, width, 0, 0).astype(F32).astype(BF16)
     own_rows = pl.ds(pl.multiple_of(t * width, width), width)
-    grads_all[s, own_rows, :] = dot_nt(ones, grads_ref[...]).astype(BF16)
-    acts_all[s, own_rows, :] = dot_nt(ones, acts_ref[...]).astype(BF16)
+    grads_all[s, own_rows, :] = grads_ref[...]
+    acts_all[s, own_rows, :] = acts_ref[...]
     pl.semaphore_wait(barrier, len(peers))
 
     grads.start()
@@ -344,56 +339,78 @@
         grads.line(k)
         grads.second(k - 1)
     grads.second(n - 1)
+    for k in range(n):
+        grads.third(k)
     acts.start()
+    for k in range(n, 2 * n):
+        grads.third(k)
+    grads.sibling(0, 4 * n)
+
+    every = range(shards)
+    norms = {}
+
+    def damp_grads():
+        norms["grads"] = damp(cov, factor, damping_ref[1])
+
+    def project(k):
+        projected[k] = dot_nn(grad_low[...], grads_all[k]).astype(BF16)
+
+    def lower():
+        grad_low[...] = grad_work[...].astype(BF16)
+
+    work = [
+        functools.partial(cov_tile, grads_all, cov, every, i, j, False)
+        for i in range(TILES)
+        for j in range(TILES)
+    ]
+    work += [damp_grads]
+    work += horner_steps(factor, grad_work, coeffs_ref, t * width, lambda: norms["grads"])
+    work += [lower]
+    work += [functools.partial(project, k) for k in every]
+    relays = []
     for k in range(1, n):
-        acts.line(k)
-        acts.second(k - 1)
-        grads.third(2 * k - 2)
-        grads.third(2 * k - 1)
-    acts.second(n - 1)
-    for k in range(2 * n - 2, 2 * n):
-        grads.third(k)
-    grads.sibling()
-    third = 0
+        relays += [functools.partial(acts.line, k), functools.partial(acts.second, k - 1)]
+    relays += [functools.partial(acts.second, n - 1)]
+    relays += [functools.partial(acts.third, k) for k in range(n)]
+    done = 0
+    for index, chunk in enumerate(work):
+        chunk()
+        upto = (index + 1) * len(relays) // len(work)
+        for relay in relays[done:upto]:
+            relay()
+        done = upto
+    near = [2 * k + p.y for k in range(n)]
+    far = [2 * k + 1 - p.y for k in range(n)]
+    acts.sibling(0, 3 * n)
+    tile = cov.shape[0] // TILES
+
+    def right_rows(slabs, i, add):
+        rows = pl.ds(i * tile, tile)
+        low = jnp.concatenate([projected[k] for k in slabs], axis=1)
+        product = dot_nt(lanes(acts_all, slabs, rows), low)
+        right[rows, :] = right[rows, :] + product if add else product
+
+    third = n
     for i in range(TILES):
-        cov_rows(grads_all, cov, i)
-        acts.third(third)
-        third += 1
-    grad_norm = damp(cov, factor, damping_ref[1])
-    while third < n:
-        acts.third(third)
-        third += 1
-    horner_rows(factor, grad_work, coeffs_ref, t * width, grad_norm)
-    grad_low[...] = grad_work[...].astype(BF16)
-    acts.third(third)
-    third += 1
-
-    def project(k, carry):
-        projected[k] = dot_nn(grad_low[...], grads_all[k]).astype(BF16)
-        return carry
-
-    lax.fori_loop(0, shards, project, 0)
+        for j in range(TILES):
+            cov_tile(acts_all, cov, near, i, j, False)
+            if j % 2 == 1 and third < 2 * n:
+                acts.third(third)
+                third += 1
+        right_rows(near, i, False)
     while third < 2 * n:
         acts.third(third)
         third += 1
-    acts.sibling()
+    acts.sibling(3 * n, 4 * n)
     for i in range(TILES):
-        cov_rows(acts_all, cov, i)
+        for j in range(TILES):
+            cov_tile(acts_all, cov, far, i, j, True)
     act_norm = damp(cov, factor, damping_ref[0])
     height = weight_ref.shape[0]
-    horner_rows(factor, act_work, coeffs_ref, s * height, act_norm)
-    tile = cov.shape[0] // TILES
-    low = jnp.concatenate([projected[k] for k in range(shards)], axis=1)
-
-    def right_rows(i, carry):
-        first = pl.multiple_of(i * tile, tile)
-        left = jnp.concatenate(
-            [acts_all[k, pl.ds(first, tile), :] for k in range(shards)], axis=1
-        )
-        right[pl.ds(first, tile), :] = dot_nt(left, low)
-        return carry
-
-    lax.fori_loop(0, TILES, right_rows, 0)
+    for run in horner_steps(factor, act_work, coeffs_ref, s * height, lambda: act_norm):
+        run()
+    for i in range(TILES):
+        right_rows(far, i, True)
     update = dot_nn(act_work[...], right[...], lax.Precision.HIGHEST)
 
     started = []
@@ -432,10 +449,16 @@
     new_momentum_ref[...] = momentum
     new_weight = weight_ref[...].astype(F32) - 0.1 * momentum
 
+    low = new_weight.astype(BF16)
+    main = weight_all.shape[2]
+    rest = width - main
+    weight_all[s, :height, :] = low[:, :main]
+    ones = eye(rest, rest, 0, 0).astype(F32).astype(BF16)
+    weight_all[s, height:, :height] = dot_nt(ones, low[:, main:]).astype(BF16)
+
     def rows_of(z, y):
-        return weight_all.at[pl.ds(pl.multiple_of((z * Y_CHIPS + y) * height, height), height), :]
-
-    weight_all[pl.ds(pl.multiple_of(s * height, height), height), :] = new_weight.astype(BF16)
+        return weight_all.at[z * Y_CHIPS + y]
+
     own = rows_of(p.z, p.y)
     across = (p.z * Y_CHIPS + 1 - p.y, t)
     lines = [
@@ -449,7 +472,11 @@
         crossed.append(push(piece, piece, pairs[11], k, across))
     for copy in crossed:
         copy.wait_recv()
-    gathered_ref[...] = weight_all[...]
+    rows = jnp.concatenate([weight_all[k, :height, :] for k in range(shards)], axis=0)
+    ones = eye(main, main, 0, 0).astype(F32).astype(BF16)
+    gathered_ref[:main, :] = dot_nt(ones, rows).astype(BF16)
+    for k in range(shards):
+        gathered_ref[main:, k * height : (k + 1) * height] = weight_all[k, height:, :height]
     for copy in started:
         copy.wait_send()
     grads.finish()
@@ -467,11 +494,11 @@
     sems = []
     for count in counts:
         sems += [pltpu.SemaphoreType.DMA((count,))] * 2
-    return pl.pallas_call(
+    new_momentum, gathered = pl.pallas_call(
         functools.partial(step_kernel, shards),
         out_shape=(
             jax.ShapeDtypeStruct((height, width), F32),
-            jax.ShapeDtypeStruct((d, width), BF16),
+            jax.ShapeDtypeStruct((width, d), BF16),
         ),
         in_specs=[vmem, vmem, vmem, vmem, smem, smem],
         out_specs=(vmem, vmem),
@@ -485,7 +512,7 @@
             pltpu.VMEM((height, d), F32),
             pltpu.VMEM((shards, width, tokens), BF16),
             pltpu.VMEM((d, width), F32),
-            pltpu.VMEM((d, width), BF16),
+            pltpu.VMEM((shards, height + width % 128, width // 128 * 128), BF16),
             pltpu.VMEM((shards, 8, 128), F32),
             pltpu.VMEM((tensors, 8, 128), F32),
         ]
@@ -493,7 +520,8 @@
         compiler_params=pltpu.CompilerParams(
             collective_id=0, has_side_effects=True, vmem_limit_bytes=56 * 2**20
         ),
-    )(acts, outgrads, weight, momentum, damping, coeffs)
+    )(acts.T, outgrads.T, weight, momentum, damping, coeffs)
+    return new_momentum, gathered.T
 
 
 def solution(mesh):

time: 116 us -> 98.6 us (0.85)
  Pallas kernels: 110 us -> 94.2 us
  local copies, waits for them, and re-layouts: 5.6 us -> 3.61 us
    pallas_call x1, Pallas kernels: 110 us -> 94.2 us  [on_device_whole(): pl.pallas_call(functools.partial(step_kernel, shards), out_shape=(jax.Sha...]
    pallas_call x1 -> x0, local copies, waits for them, and re-layouts: 2.33 us -> none  [on_device_whole(): pl.pallas_call(functools.partial(step_kernel, shards), out_shape=(jax.Sha...]
    unnamed x7 -> x2, local copies, waits for them, and re-layouts: 3.27 us -> 3.61 us
where the time goes in v2:
time: 98.6 us; the launch traced here: 98.4 us
  Pallas kernels  94.2 us (96%)
  local copies, waits for them, and re-layouts  3.61 us (4%)
    pallas_call x1, Pallas kernels, on_device_whole(): pl.pallas_call(functools.partial(step_kernel, shards), out_shape=(jax.Sha...  94.2 us
    unnamed x2, local copies, waits for them, and re-layouts  3.61 us

profile of v2, /device:TPU:0, one launch (start us, length us, event | category | flops | bytes accessed | tf_op | source)
XLA Modules:
  0.0 98.4 jit_solution(1475358419729145285)
XLA Ops:
  0.6 94.2 %shard_map.77 = (f32[144,288]{1,0:T(8,128)}, bf16[288,1152]{1,0:T(8,128)(2,1)}) custom-call(bf16[288,256]{1,0:T(8,128)(2,1)} %bitcast.4, bf16[288,256]{1,0:T(8,128)(2,1)} %bitcast.5, bf16[144,288]{1,0:T(8,128)(2,1)} %weight_ref.1, f32[144,288]{1,0:T(8,128)} %momentum_ref.1, f32[2]{0:T(128)} %damping_ref.1, f32[4]{0:T(128)} %coeffs_ref.1), custom_call_target="tpu_custom_call" | custom-call | tf_op jit(solution)/shard_map/pallas_call | solution.py:497
  94.8 1.6 %copy.10 = f32[144,288]{1,0:T(8,128)} copy(f32[144,288]{1,0:T(8,128)} %get-tuple-element.8) | data formatting | bytes 331776
  96.4 2.0 %copy.11 = bf16[1152,288]{0,1:T(8,128)(2,1)} copy(bf16[1152,288]{0,1:T(8,128)(2,1)} %bitcast.3) | data formatting | bytes 1327104

commit v3 on v2

--- a/solution.py
+++ b/solution.py
@@ -253,16 +253,23 @@
         trace = trace + total(jnp.where(eye(step, step, 0, 0), part, 0.0))
     shift = damping * trace / d
 
-    def rows(i, acc):
-        first = pl.multiple_of(i * step, step)
-        piece = cov[pl.ds(first, step), :]
-        diag = eye(step, d, first, 0)
-        piece = (piece + jnp.where(diag, shift, 0.0)).astype(BF16)
-        factor[pl.ds(first, step), :] = piece
-        wide = piece.astype(F32)
-        return acc + jnp.sum(wide * wide, axis=0, keepdims=True)
-
-    squares = lax.fori_loop(0, 9, rows, jnp.zeros((1, d), F32))
+    tile = d // TILES
+    unit = eye(tile, tile, 0, 0)
+    ones = unit.astype(F32).astype(BF16)
+    squares = jnp.zeros((1, tile), F32)
+    for i in range(TILES):
+        for j in range(i, TILES):
+            rows, cols = slice(i * tile, (i + 1) * tile), slice(j * tile, (j + 1) * tile)
+            piece = cov[rows, cols]
+            if i == j:
+                piece = piece + jnp.where(unit, shift, 0.0)
+            low = piece.astype(BF16)
+            factor[rows, cols] = low
+            wide = low.astype(F32)
+            square = jnp.sum(wide * wide, axis=0, keepdims=True)
+            squares = squares + (square if i == j else 2.0 * square)
+            if i != j:
+                factor[cols, rows] = dot_nt(ones, low).astype(BF16)
     return jnp.sqrt(jnp.sum(squares, axis=1, keepdims=True))
 
 
@@ -361,7 +368,7 @@
     work = [
         functools.partial(cov_tile, grads_all, cov, every, i, j, False)
         for i in range(TILES)
-        for j in range(TILES)
+        for j in range(i, TILES)
     ]
     work += [damp_grads]
     work += horner_steps(factor, grad_work, coeffs_ref, t * width, lambda: norms["grads"])
@@ -392,9 +399,9 @@
 
     third = n
     for i in range(TILES):
-        for j in range(TILES):
+        for j in range(i, TILES):
             cov_tile(acts_all, cov, near, i, j, False)
-            if j % 2 == 1 and third < 2 * n:
+            if i + j > 0 and third < 2 * n:
                 acts.third(third)
                 third += 1
         right_rows(near, i, False)
@@ -403,7 +410,7 @@
         third += 1
     acts.sibling(3 * n, 4 * n)
     for i in range(TILES):
-        for j in range(TILES):
+        for j in range(i, TILES):
             cov_tile(acts_all, cov, far, i, j, True)
     act_norm = damp(cov, factor, damping_ref[0])
     height = weight_ref.shape[0]

time: 98.6 us -> 92.6 us (0.939)
  Pallas kernels: 94.2 us -> 88.1 us
    pallas_call x1, Pallas kernels: 94.2 us -> 88.1 us  [on_device_whole(): pl.pallas_call(functools.partial(step_kernel, shards), out_shape=(jax.Sha...]
where the time goes in v3:
time: 92.6 us; the launch traced here: 92.4 us
  Pallas kernels  88.1 us (95%)
  local copies, waits for them, and re-layouts  3.61 us (4%)
    pallas_call x1, Pallas kernels, on_device_whole(): pl.pallas_call(functools.partial(step_kernel, shards), out_shape=(jax.Sha...  88.1 us
    unnamed x2, local copies, waits for them, and re-layouts  3.61 us

profile of v3, /device:TPU:0, one launch (start us, length us, event | category | flops | bytes accessed | tf_op | source)
XLA Modules:
  0.0 92.4 jit_solution(17958234435065348425)
XLA Ops:
  0.6 88.1 %shard_map.77 = (f32[144,288]{1,0:T(8,128)}, bf16[288,1152]{1,0:T(8,128)(2,1)}) custom-call(bf16[288,256]{1,0:T(8,128)(2,1)} %bitcast.4, bf16[288,256]{1,0:T(8,128)(2,1)} %bitcast.5, bf16[144,288]{1,0:T(8,128)(2,1)} %weight_ref.1, f32[144,288]{1,0:T(8,128)} %momentum_ref.1, f32[2]{0:T(128)} %damping_ref.1, f32[4]{0:T(128)} %coeffs_ref.1), custom_call_target="tpu_custom_call" | custom-call | tf_op jit(solution)/shard_map/pallas_call | solution.py:504
  88.8 1.6 %copy.10 = f32[144,288]{1,0:T(8,128)} copy(f32[144,288]{1,0:T(8,128)} %get-tuple-element.8) | data formatting | bytes 331776
  90.4 2.0 %copy.11 = bf16[1152,288]{0,1:T(8,128)(2,1)} copy(bf16[1152,288]{0,1:T(8,128)(2,1)} %bitcast.3) | data formatting | bytes 1327104
